TPU v7x, 32 devices: a whole 2x2x4 slice. The times are simulated.
32 devices in a mesh: filt: 16 (over z, y, x), depth: 2 (over core).
Axes of the slice: x: 2, y: 2, z: 4, core: 2. Of those that a mesh axis runs over, the one named last changes fastest.
Arguments:
- volume: bfloat16 [256, 8, 64, 128], P(None, 'depth', 'filt'), may hold values from -6 to 6
- weights: bfloat16 [128, 27, 256], P('filt'), may hold values from -0.078125 to 0.078125
- bias: float32 [128], replicated, may hold values from -3 to 3
- grad_out: bfloat16 [128, 8, 64, 128], P(None, 'depth', 'filt'), may hold values from -0.0234375 to 0.0234375
Outputs:
- output: bfloat16 [128, 8, 64, 128], P(None, 'depth', 'filt')
- grad_w: float32 [128, 27, 256], P('filt')
All inputs are finite; a program needn't handle non-finite values.
Results may differ from a plain program's by a relative error of at most 0.001.
Values may be sent and summed in bfloat16 or wider, within the bound.
A program may use at most 64 MiB of HBM per device.

v0:
```python
import jax
import jax.numpy as jnp
from jax import lax
from jax.sharding import PartitionSpec as P


def padded_2(block, sides, width):
    for axis, dim in sides:
        count = lax.axis_size(axis)
        forward = [(i, i + 1) for i in range(count - 1)]
        backward = [(target, source) for source, target in forward]
        low = lax.ppermute(
            lax.slice_in_dim(block, block.shape[dim] - width, None, axis=dim), axis, forward
        )
        high = lax.ppermute(lax.slice_in_dim(block, 0, width, axis=dim), axis, backward)
        block = jnp.concatenate([low, block, high], axis=dim)
    return block


def body(volume, weights, bias, grad_out):
    channels = volume.shape[0]
    rimmed = padded_2(volume, (("filt", 2), ("depth", 1)), 1)
    padded = jnp.pad(rimmed, ((0, 0), (0, 0), (0, 0), (1, 1)))
    stacked = padded[None]
    per_channel = padded[:, None]
    piece = lax.all_gather(weights, "filt", axis=0, tiled=True)
    count = piece.shape[0]
    kernel = piece.reshape(count, 3, 3, 3, channels)
    result = lax.conv_general_dilated(
        stacked,
        kernel,
        (1, 1, 1),
        "VALID",
        dimension_numbers=("NCDHW", "ODHWI", "NCDHW"),
        preferred_element_type=jnp.float32,
    )
    total = result[0]
    output = (total + bias[:, None, None, None]).astype(jnp.bfloat16)
    all_filters = grad_out.shape[0]
    cotangent = grad_out[:, None]
    taps = lax.conv_general_dilated(
        per_channel,
        cotangent,
        (1, 1, 1),
        "VALID",
        dimension_numbers=("NCDHW", "OIDHW", "CDHWN"),
        preferred_element_type=jnp.float32,
    )
    term = taps.reshape(all_filters, 27, channels)
    summed = lax.psum(term, "depth")
    grad_w = lax.psum_scatter(summed, "filt", scatter_dimension=0, tiled=True)
    return (output, grad_w)


def solution(mesh):
    in_specs = (
        P(None, "depth", "filt", None),
        P("filt", None, None),
        P(),
        P(None, "depth", "filt", None),
    )
    out_specs = (P(None, "depth", "filt", None), P("filt", None, None))
    return jax.shard_map(body, mesh=mesh, in_specs=in_specs, out_specs=out_specs, check_vma=False)
```

profile of v0, /device:TPU:0, one launch (start us, length us, event | category | flops | bytes accessed | tf_op | source)
XLA Modules:
  0.0 207.8 jit_solution(15170670044726231992)
XLA Ops:
  7.2 0.0 all-gather.2.cloned.1.call-start
  7.2 1.6 copy.11
  8.9 4.9 %collective-permute-start = (bf16[256,4,1,128]{0,3,2,1:T(8,128)(2,1)S(1)}, bf16[256,4,1,128]{0,3,2,1:T(8,128)(2,1)S(1)}, u32[]{:S(2)}, u32[]{:S(2)}) collective-permute-start(bf16[256,4,1,128]{0,3,2,1:T(8,128)(2,1)S(1)} %get-tuple-element.6), channel_id=1, source_target_pairs={{0,2},{2,4},{4,6},{6,8},{8,10},{10,12},{12,14},{14,16},{16,18},{18... | collective-permute-start | bytes 786440 | tf_op jit(solution)/shard_map/ppermute | solution.py:12
  13.8 1.3 collective-permute-start.1
  15.1 9.9 %collective-permute-done = bf16[256,4,1,128]{0,3,2,1:T(8,128)(2,1)S(1)} collective-permute-done((bf16[256,4,1,128]{0,3,2,1:T(8,128)(2,1)S(1)}, bf16[256,4,1,128]{0,3,2,1:T(8,128)(2,1)S(1)}, u32[]{:S(2)}, u32[]{:S(2)}) %collective-permute-start) | collective-permute-done | bytes 262176 | tf_op jit(solution)/shard_map/ppermute | solution.py:12
  25.0 1.9 collective-permute-done.1
  26.9 1.0 pad_maximum_fusion.2
  27.8 1.3 collective-permute-start.2
  29.1 1.3 collective-permute-start.3
  30.4 0.0 all-gather.2.cloned.1.call-update
  30.5 0.0 reduce-scatter.2.cloned.1.call-start
  30.5 2.7 %copy.18 = bf16[128,1,4,4,128]{0,1,4,3,2:T(2,128)(2,1)S(1)} copy(bf16[128,1,4,4,128]{4,3,2,0,1:T(4,128)(2,1)} %bitcast.30) | data formatting | bytes 1048576 | tf_op jit(solution)/shard_map/broadcast_in_dim | solution.py:40
  33.2 0.0 collective-permute-done.2
  33.2 0.0 collective-permute-done.3
  33.2 1.2 fusion.28
  34.4 32.6 %fusion.2 = f32[128,3,3,3,256]{4,0,3,2,1:T(8,128)} fusion(bf16[128,1,4,4,128]{0,1,4,3,2:T(2,128)(2,1)S(1)} %copy.18, bf16[256,1,6,6,130]{0,4,3,2,1:T(8,128)(2,1)S(1)} %fusion.28), kind=kOutput, calls=%fused_computation.5 | convolution fusion | flops 3623878656 | bytes 6459392 | tf_op jit(solution)/shard_map/conv_general_dilated | solution.py:41
  67.0 0.0 reduce-scatter.2.cloned.1.call-update
  67.0 0.0 all-reduce.3.cloned.1.call-start
  67.0 1.2 fusion.29
  68.2 1.6 pad.5
  69.9 3.7 %reshape.15 = bf16[256,6,6,1,8,17]{0,5,4,2,1,3:T(8,128)(2,1)S(1)} reshape(bf16[256,6,6,1,136]{0,4,2,1,3:T(8,128)(2,1)} %pad.5) | data formatting | bytes 5013504 | tf_op jit(solution)/shard_map/conv_general_dilated | solution.py:29
  73.6 0.0 copy-start.1
  73.6 2.2 %copy.15 = bf16[256,6,6,1,8,17]{0,4,5,2,1,3:T(8,128)(2,1)} copy(bf16[256,6,6,1,8,17]{0,5,4,2,1,3:T(8,128)(2,1)S(1)} %reshape.15) | data formatting | bytes 5013504 | tf_op jit(solution)/shard_map/conv_general_dilated | solution.py:29
  75.8 1.0 slice.20
  76.9 17.5 %all-gather.2.cloned.1.call-done = bf16[128,27,256]{2,0,1:T(8,128)(2,1)} async-done(((bf16[8,27,256]{2,0,1:T(8,128)(2,1)}), bf16[128,27,256]{2,0,1:T(8,128)(2,1)}) %all-gather.2.cloned.1.call-update) | async-done | bytes 1769488 | tf_op jit(solution)/shard_map/all_gather | solution.py:26
  94.4 0.0 copy-done.1
  94.4 0.0 copy-start
  94.4 10.4 %fusion.17 = f32[4,4,8,17,128]{4,2,3,1,0:T(8,128)S(1)} fusion(bf16[128,3,3,3,256]{4,0,3,2,1:T(8,128)(2,1)} %bitcast.31, bf16[256,6,6,1,7,2]{0,4,5,2,1,3:T(8,128)(2,1)S(1)} %slice.20, bf16[256,6,6,1,8,17]{0,4,5,2,1,3:T(8,128)(2,1)} %copy.15, pred[8,17]{0,1:T(8,128)(4,1)S(1)} %copy-done.1), kind=kOutput, calls=%fused_computation.21 | convolution fusion | flops 3859054592 | bytes 5648520 | tf_op jit(solution)/shard_map/conv_general_dilated | solution.py:29
  104.8 0.3 copy.16
  105.1 75.7 %reduce-scatter.2.cloned.1.call-done = f32[8,27,256]{2,0,1:T(8,128)} async-done(((f32[128,27,256]{2,0,1:T(8,128)}), f32[8,27,256]{2,0,1:T(8,128)}) %reduce-scatter.2.cloned.1.call-update) | async-done | bytes 221200 | tf_op jit(solution)/shard_map/reduce_scatter | solution.py:51
  180.8 0.0 all-reduce.3.cloned.1.call-update
  180.8 0.0 copy-done
  180.8 0.2 fusion.21
  181.0 1.1 copy.20
  182.1 17.5 %all-reduce.3.cloned.1.call-done = f32[8,27,256]{2,0,1:T(8,128)} async-done(((f32[8,27,256]{2,0,1:T(8,128)}), f32[8,27,256]{2,0,1:T(8,128)}) %all-reduce.3.cloned.1.call-update) | async-done | bytes 221200 | tf_op jit(solution)/shard_map/psum | solution.py:50
  199.7 1.6 copy.24
  (1 shorter events, 0.0 us)
Async XLA Ops:
  7.2 87.2 %all-gather.2.cloned.1.call-start = ((), (), s32[]{:S(2)}) async-start(), calls=%async_computation.1 | async-start | bytes 1880064 | tf_op jit(solution)/shard_map/all_gather | solution.py:26
  8.9 16.0 %collective-permute-start = (bf16[256,4,1,128]{0,3,2,1:T(8,128)(2,1)S(1)}, bf16[256,4,1,128]{0,3,2,1:T(8,128)(2,1)S(1)}, u32[]{:S(2)}, u32[]{:S(2)}) collective-permute-start(bf16[256,4,1,128]{0,3,2,1:T(8,128)(2,1)S(1)} %get-tuple-element.6), channel_id=1, source_target_pairs={{0,2},{2,4},{4,6},{6,8},{8,10},{10,12},{12,14},{14,16},{16,18},{18... | collective-permute-start | bytes 786440 | tf_op jit(solution)/shard_map/ppermute | solution.py:12
  13.8 13.1 %collective-permute-start.1 = (bf16[256,4,1,128]{0,3,2,1:T(8,128)(2,1)S(1)}, bf16[256,4,1,128]{0,3,2,1:T(8,128)(2,1)S(1)}, u32[]{:S(2)}, u32[]{:S(2)}) collective-permute-start(bf16[256,4,1,128]{0,3,2,1:T(8,128)(2,1)S(1)} %get-tuple-element.7), channel_id=1, source_target_pairs={{2,0},{4,2},{6,4},{8,6},{10,8},{12,10},{14,12},{16,14},{18,16},{20... | collective-permute-start | bytes 786440 | tf_op jit(solution)/shard_map/ppermute | solution.py:15
  27.8 5.3 %collective-permute-start.2 = (bf16[256,1,6,128]{0,3,2,1:T(8,128)(2,1)}, bf16[256,1,6,128]{0,3,2,1:T(8,128)(2,1)S(1)}, u32[]{:S(2)}, u32[]{:S(2)}) collective-permute-start(bf16[256,1,6,128]{0,3,2,1:T(8,128)(2,1)} %get-tuple-element.4), channel_id=1, source_target_pairs={{0,1},{2,3},{4,5},{6,7},{8,9},{10,11},{12,13},{14,15},{16,17},{18,... | collective-permute-start | bytes 1179656 | tf_op jit(solution)/shard_map/ppermute | solution.py:12
  29.1 4.0 %collective-permute-start.3 = (bf16[256,1,6,128]{0,3,2,1:T(8,128)(2,1)}, bf16[256,1,6,128]{0,3,2,1:T(8,128)(2,1)S(1)}, u32[]{:S(2)}, u32[]{:S(2)}) collective-permute-start(bf16[256,1,6,128]{0,3,2,1:T(8,128)(2,1)} %get-tuple-element.5), channel_id=1, source_target_pairs={{1,0},{3,2},{5,4},{7,6},{9,8},{11,10},{13,12},{15,14},{17,16},{19,... | collective-permute-start | bytes 1179656 | tf_op jit(solution)/shard_map/ppermute | solution.py:15
  30.5 150.3 %reduce-scatter.2.cloned.1.call-start = ((), (), s32[]{:S(2)}) async-start(), calls=%async_computation.2 | async-start | bytes 3760128 | tf_op jit(solution)/shard_map/reduce_scatter | solution.py:51
  67.0 132.7 %all-reduce.3.cloned.1.call-start = ((), (), s32[]{:S(2)}) async-start(), calls=%async_computation.3 | async-start | bytes 442368 | tf_op jit(solution)/shard_map/psum | solution.py:50
  73.6 20.8 %copy-start.1 = (pred[8,17]{0,1:T(8,128)(4,1)S(1)}, pred[8,17]{0,1:T(8,128)(4,1)}, u32[]{:S(2)}) copy-start(pred[8,17]{0,1:T(8,128)(4,1)} %constant.12) | copy-start | bytes 412
  94.4 86.4 %copy-start = (f32[128]{0:T(128)S(1)}, f32[128]{0:T(128)}, u32[]{:S(2)}) copy-start(f32[128]{0:T(128)} %param.6) | copy-start | bytes 1540
Sparse Core Ops, SparseCore 0:
  30.6 63.7 all-gather.1
  96.7 84.0 reduce-scatter.1
  183.1 16.5 all-reduce.2
where the time goes:
time: 208 us
  waiting for transfers between devices  123 us (59%)
  matrix products  43 us (21%)
  local copies, waits for them, and re-layouts  16 us (8%)
  between operations  13.9 us (7%)
  starting transfers between devices  8.87 us (4%)
  other arithmetic  3.51 us (2%)
    reduce_scatter x1, waiting for transfers between devices, body(): grad_w = lax.psum_scatter(summed, 'filt', scatter_dimension=0, tiled=True)  75.7 us
    conv_general_dilated x1, matrix products, body(): lax.conv_general_dilated(per_channel, cotangent, (1, 1, 1), 'VALID', dime...  32.6 us
    psum x1, waiting for transfers between devices, body(): summed = lax.psum(term, 'depth')  17.5 us
    all_gather x1, waiting for transfers between devices, body(): piece = lax.all_gather(weights, 'filt', axis=0, tiled=True)  17.5 us
    conv_general_dilated x1, matrix products, body(): lax.conv_general_dilated(stacked, kernel, (1, 1, 1), 'VALID', dimension_n...  10.4 us
    ppermute x2, waiting for transfers between devices, padded_2(): lax.ppermute(lax.slice_in_dim(block, block.shape[dim] - width, None, axis...  9.88 us
    conv_general_dilated x4, local copies, waits for them, and re-layouts, body(): lax.conv_general_dilated(stacked, kernel, (1, 1, 1), 'VALID', dimension_n...  7.27 us
    ppermute x2, starting transfers between devices, padded_2(): lax.ppermute(lax.slice_in_dim(block, block.shape[dim] - width, None, axis...  6.16 us
  transfers between devices with their start and end apart: 7, of which 5 were waited for; matrix products, arithmetic and copies ran while one was open for 28% of the time, Pallas kernels for 0%

commit v1 on v0

--- a/solution.py
+++ b/solution.py
@@ -1,7 +1,13 @@
 import jax
 import jax.numpy as jnp
 from jax import lax
+from jax.experimental import pallas as pl
+from jax.experimental.pallas import tpu as pltpu
 from jax.sharding import PartitionSpec as P
+
+F32 = jnp.float32
+BF16 = jnp.bfloat16
+MESH = pl.DeviceIdType.MESH
 
 
 def padded_2(block, sides, width):
@@ -17,7 +23,7 @@
     return block
 
 
-def body(volume, weights, bias, grad_out):
+def general_body(volume, weights, bias, grad_out):
     channels = volume.shape[0]
     rimmed = padded_2(volume, (("filt", 2), ("depth", 1)), 1)
     padded = jnp.pad(rimmed, ((0, 0), (0, 0), (0, 0), (1, 1)))
@@ -34,13 +40,11 @@
         dimension_numbers=("NCDHW", "ODHWI", "NCDHW"),
         preferred_element_type=jnp.float32,
     )
-    total = result[0]
-    output = (total + bias[:, None, None, None]).astype(jnp.bfloat16)
+    output = (result[0] + bias[:, None, None, None]).astype(jnp.bfloat16)
     all_filters = grad_out.shape[0]
-    cotangent = grad_out[:, None]
     taps = lax.conv_general_dilated(
         per_channel,
-        cotangent,
+        grad_out[:, None],
         (1, 1, 1),
         "VALID",
         dimension_numbers=("NCDHW", "OIDHW", "CDHWN"),
@@ -52,6 +56,308 @@
     return (output, grad_w)
 
 
+def fused_kernel(
+    v_ref, w_ref, b_ref, g_ref,
+    out_ref, gw_ref,
+    vp, g3, wg, w9, part, ra, b1, b2, b3, gs,
+    hs, hr, ws, wr, rs_s, rs_r, zs, zr,
+):
+    me = lax.axis_index("filt")
+    core = lax.axis_index("depth")
+    other = 1 - core
+    xi = me % 2
+    yi = (me // 2) % 2
+    zi = me // 4
+    x_peer = me + 1 - 2 * xi
+    y_peer = me + 2 - 4 * yi
+    z_to = [(zi + k) % 4 for k in (1, 2, 3)]
+    z_peer = [t * 4 + yi * 2 + xi for t in z_to]
+    left, right = me - 1, me + 1
+
+    def dev(filt, depth=None):
+        return {"filt": filt, "depth": core if depth is None else depth}
+
+    def copy(src, dst, s_sem, r_sem, device):
+        return pltpu.make_async_remote_copy(
+            src_ref=src, dst_ref=dst, send_sem=s_sem, recv_sem=r_sem,
+            device_id=device, device_id_type=MESH,
+        )
+
+    barrier = pltpu.get_barrier_semaphore()
+
+    def greet(device):
+        pl.semaphore_signal(barrier, inc=1, device_id=device, device_id_type=MESH)
+
+    greet(dev(me, other))
+    greet(dev(x_peer))
+    greet(dev(y_peer))
+    for p in z_peer:
+        greet(dev(p))
+
+    @pl.when(me > 0)
+    def _():
+        greet(dev(left))
+
+    @pl.when(me < 15)
+    def _():
+        greet(dev(right))
+
+    pl.semaphore_wait(barrier, 6 + jnp.minimum(me, 1) + jnp.minimum(15 - me, 1))
+
+    to_right = copy(v_ref.at[:, :, 384:512], vp.at[1:5, :, 0:128], hs.at[0], hr.at[0], dev(right))
+    to_left = copy(v_ref.at[:, :, 0:128], vp.at[1:5, :, 640:768], hs.at[1], hr.at[1], dev(left))
+
+    @pl.when(me < 15)
+    def _():
+        to_right.start()
+
+    @pl.when(me > 0)
+    def _():
+        to_left.start()
+
+    my_edge = 3 - 3 * core
+    there = 5 * core
+    send_slot = 5 - 5 * other
+    inner = copy(v_ref.at[my_edge], vp.at[send_slot, :, 128:640], hs.at[2], hr.at[2], dev(me, other))
+    inner.start()
+
+    wg[core, zi, yi, xi] = w_ref[core]
+    for k in range(3):
+        copy(w_ref.at[core], wg.at[core, zi, yi, xi], ws.at[k], wr.at[k], dev(z_peer[k])).start()
+
+    vp[1:5, :, 128:640] = v_ref[...]
+    empty = 5 - 5 * (1 - core)
+    vp[empty] = jnp.zeros((256, 768), BF16)
+
+    @pl.when(me == 0)
+    def _():
+        vp[1:5, :, 0:128] = jnp.zeros((4, 256, 128), BF16)
+        vp[send_zero_slot(core), :, 0:128] = jnp.zeros((256, 128), BF16)
+
+    @pl.when(me == 15)
+    def _():
+        vp[1:5, :, 640:768] = jnp.zeros((4, 256, 128), BF16)
+        vp[send_zero_slot(core), :, 640:768] = jnp.zeros((256, 128), BF16)
+
+    lane = lax.broadcasted_iota(jnp.int32, (128, 128), 1)
+    for z in range(4):
+        for x in range(4):
+            cols = slice(x * 128, x * 128 + 128)
+            g = g_ref[z, :, cols]
+            gf = g.astype(F32)
+            up = jnp.where(lane == 127, 0.0, pltpu.roll(gf, 127, 1))
+            down = jnp.where(lane == 0, 0.0, pltpu.roll(gf, 1, 1))
+            g3[z, 0:128, cols] = up.astype(BF16)
+            g3[z, 128:256, cols] = g
+            g3[z, 256:384, cols] = down.astype(BF16)
+
+    edge_slot = 4 - 3 * core
+    corner_l = copy(vp.at[edge_slot, :, 0:128], vp.at[send_slot, :, 0:128], hs.at[3], hr.at[3], dev(me, other))
+    corner_r = copy(vp.at[edge_slot, :, 640:768], vp.at[send_slot, :, 640:768], hs.at[4], hr.at[4], dev(me, other))
+
+    @pl.when(me > 0)
+    def _():
+        to_right.wait_recv()
+        corner_l.start()
+
+    @pl.when(me < 15)
+    def _():
+        to_left.wait_recv()
+        corner_r.start()
+
+    w_z = [copy(w_ref.at[core], wg.at[core, zi, yi, xi], ws.at[k], wr.at[k], dev(z_peer[k])) for k in range(3)]
+    for c in w_z:
+        c.wait_recv()
+    w_y = copy(wg.at[core, :, yi, xi], wg.at[core, :, yi, xi], ws.at[3], wr.at[3], dev(y_peer))
+    w_y.start()
+    w_x = copy(wg.at[core, :, :, xi], wg.at[core, :, :, xi], ws.at[4], wr.at[4], dev(x_peer))
+    w_c = copy(wg.at[core], wg.at[core], ws.at[5], wr.at[5], dev(me, other))
+
+    inner.wait_recv()
+
+    @pl.when(me > 0)
+    def _():
+        corner_l.wait_recv()
+
+    @pl.when(me < 15)
+    def _():
+        corner_r.wait_recv()
+
+    def grad(j):
+        dz, dx = j // 3, j % 3
+        total = None
+        for z in range(4):
+            term = lax.dot_general(
+                g3[z], vp[z + dz, :, dx * 128 : dx * 128 + 512],
+                (((1,), (1,)), ((), ())), preferred_element_type=F32,
+            )
+            total = term if total is None else total + term
+        for h in range(2):
+            part[j, h] = total[:, h * 128 : h * 128 + 128].reshape(3, 4, 2, 2, 8, 128)
+
+    def stage_a(j):
+        return copy(part.at[j, other], ra.at[j], rs_s.at[0, j], rs_r.at[0, j], dev(me, other))
+
+    def stage_1(j):
+        if j % 2 == 0:
+            return copy(ra.at[j, :, :, :, 1 - xi], b1.at[j], rs_s.at[1, j], rs_r.at[1, j], dev(x_peer))
+        return copy(ra.at[j, :, :, 1 - yi], b1.at[j], rs_s.at[1, j], rs_r.at[1, j], dev(y_peer))
+
+    def stage_2(j):
+        if j % 2 == 0:
+            return copy(b1.at[j, :, :, 1 - yi], b2.at[j], rs_s.at[2, j], rs_r.at[2, j], dev(y_peer))
+        return copy(b1.at[j, :, :, 1 - xi], b2.at[j], rs_s.at[2, j], rs_r.at[2, j], dev(x_peer))
+
+    def stage_3(j):
+        return [
+            copy(b2.at[j, :, z_to[k]], b3.at[j, k], zs.at[j, k], zr.at[j, k], dev(z_peer[k]))
+            for k in range(3)
+        ]
+
+    def after_a(j):
+        stage_a(j).wait_recv()
+        ra[j] = ra[j] + part[j, core]
+        stage_1(j).start()
+
+    def after_1(j):
+        stage_1(j).wait_recv()
+        mine = ra[j, :, :, :, xi] if j % 2 == 0 else ra[j, :, :, yi]
+        b1[j] = b1[j] + mine
+        stage_2(j).start()
+
+    def after_2(j):
+        stage_2(j).wait_recv()
+        mine = b1[j, :, :, yi] if j % 2 == 0 else b1[j, :, :, xi]
+        b2[j] = b2[j] + mine
+        for c in stage_3(j):
+            c.start()
+
+    def after_3(j):
+        for c in stage_3(j):
+            c.wait_recv()
+        gs[core, 3 * j : 3 * j + 3] = b2[j, :, zi] + b3[j, 0] + b3[j, 1] + b3[j, 2]
+
+    def arrange():
+        for h in range(2):
+            for z in range(4):
+                for y in range(2):
+                    pair = [wg[h, z, y, x].astype(F32).reshape(27, 8, 128) for x in range(2)]
+                    rows = jnp.concatenate(pair, axis=1).astype(BF16).reshape(9, 3, 16, 128)
+                    at = 16 * (2 * z + y)
+                    for dy in range(3):
+                        w9[:, dy * 128 + at : dy * 128 + at + 16, h * 128 : h * 128 + 128] = rows[:, dy]
+
+    def forward(u):
+        z, half = u // 2, u % 2
+        total = None
+        for dz in range(3):
+            for dx in range(3):
+                at = (dx + 2 * half) * 128
+                term = jnp.dot(w9[dz * 3 + dx], vp[z + dz, :, at : at + 256], preferred_element_type=F32)
+                total = term if total is None else total + term
+        for x in range(2):
+            cols = slice(x * 128, x * 128 + 128)
+            low = jnp.where(lane == 0, 0.0, pltpu.roll(total[0:128, cols], 1, 1))
+            high = jnp.where(lane == 127, 0.0, pltpu.roll(total[256:384, cols], 127, 1))
+            value = low + total[128:256, cols] + high + b_ref[...]
+            at = (x + 2 * half) * 128
+            out_ref[z, :, at : at + 128] = value.astype(BF16)
+
+    for t in range(9):
+        grad(t)
+        stage_a(t).start()
+        if t >= 1:
+            after_a(t - 1)
+        if t == 3:
+            w_y.wait_recv()
+            w_x.start()
+        if t >= 5:
+            after_1(t - 5)
+    after_a(8)
+    w_x.wait_recv()
+    w_c.start()
+    after_1(4)
+    after_2(0)
+    w_c.wait_recv()
+    arrange()
+    for u in range(8):
+        forward(u)
+        if u < 4:
+            after_1(5 + u)
+        after_2(1 + u)
+        if u >= 3:
+            after_3(u - 3)
+    for j in range(5, 9):
+        after_3(j)
+    last = copy(gs.at[core], gs.at[core], hs.at[5], hr.at[5], dev(me, other))
+    last.start()
+    gw_ref[core] = gs[core]
+
+    @pl.when(me < 15)
+    def _():
+        to_right.wait_send()
+        corner_r.wait_send()
+
+    @pl.when(me > 0)
+    def _():
+        to_left.wait_send()
+        corner_l.wait_send()
+
+    inner.wait_send()
+    for c in w_z + [w_y, w_x, w_c]:
+        c.wait_send()
+    for j in range(9):
+        stage_a(j).wait_send()
+        stage_1(j).wait_send()
+        stage_2(j).wait_send()
+        for c in stage_3(j):
+            c.wait_send()
+    last.wait()
+    gw_ref[other] = gs[other]
+
+
+def send_zero_slot(core):
+    return 5 - 5 * core
+
+
+def fused_body(volume, weights, bias, grad_out):
+    v = volume.transpose(1, 0, 2, 3).reshape(4, 256, 512)
+    g = grad_out.transpose(1, 0, 2, 3).reshape(4, 128, 512)
+    w = weights.reshape(8, 27, 2, 128).transpose(2, 1, 0, 3).reshape(2, 216, 128)
+    b = jnp.broadcast_to(bias[:, None], (128, 128))
+    vmem = pl.BlockSpec(memory_space=pltpu.VMEM)
+    dma = pltpu.SemaphoreType.DMA
+    out, gw = pl.pallas_call(
+        fused_kernel,
+        out_shape=(
+            jax.ShapeDtypeStruct((4, 128, 512), BF16),
+            jax.ShapeDtypeStruct((2, 27, 8, 128), F32),
+        ),
+        in_specs=[vmem] * 4,
+        out_specs=(vmem, vmem),
+        scratch_shapes=[
+            pltpu.VMEM((6, 256, 768), BF16),
+            pltpu.VMEM((4, 384, 512), BF16),
+            pltpu.VMEM((2, 4, 2, 2, 216, 128), BF16),
+            pltpu.VMEM((9, 384, 256), BF16),
+            pltpu.VMEM((9, 2, 3, 4, 2, 2, 8, 128), F32),
+            pltpu.VMEM((9, 3, 4, 2, 2, 8, 128), F32),
+            pltpu.VMEM((9, 3, 4, 2, 8, 128), F32),
+            pltpu.VMEM((9, 3, 4, 8, 128), F32),
+            pltpu.VMEM((9, 3, 3, 8, 128), F32),
+            pltpu.VMEM((2, 27, 8, 128), F32),
+            dma((6,)), dma((6,)), dma((6,)), dma((6,)),
+            dma((3, 9)), dma((3, 9)), dma((9, 3)), dma((9, 3)),
+        ],
+        compiler_params=pltpu.CompilerParams(
+            collective_id=0, has_side_effects=True, vmem_limit_bytes=48 << 20
+        ),
+    )(v, w, b, g)
+    output = out.reshape(4, 128, 4, 128).transpose(1, 0, 2, 3)
+    grad_w = gw.transpose(2, 1, 0, 3).reshape(8, 27, 256)
+    return (output, grad_w)
+
+
 def solution(mesh):
     in_specs = (
         P(None, "depth", "filt", None),
@@ -60,4 +366,12 @@
         P(None, "depth", "filt", None),
     )
     out_specs = (P(None, "depth", "filt", None), P("filt", None, None))
+    small = mesh.shape["filt"] == 16 and mesh.shape["depth"] == 2
+
+    def body(volume, weights, bias, grad_out):
+        shapes = (volume.shape, weights.shape, grad_out.shape)
+        if small and shapes == ((256, 4, 4, 128), (8, 27, 256), (128, 4, 4, 128)):
+            return fused_body(volume, weights, bias, grad_out)
+        return general_body(volume, weights, bias, grad_out)
+
     return jax.shard_map(body, mesh=mesh, in_specs=in_specs, out_specs=out_specs, check_vma=False)

time: 208 us -> 62.3 us (0.30)
  waiting for transfers between devices: 123 us -> 0 us
  Pallas kernels: 0 us -> 56 us
  matrix products: 43 us -> 0 us
  between operations: 13.9 us -> 0.71 us
  local copies, waits for them, and re-layouts: 16 us -> 5.35 us
  starting transfers between devices: 8.87 us -> 0 us
  other arithmetic: 3.51 us -> 0 us
    reduce_scatter x1 -> x0, waiting for transfers between devices: 75.7 us -> none  [body(): grad_w = lax.psum_scatter(summed, 'filt', scatter_dimension=0, tiled=True)]
    pallas_call x0 -> x1, Pallas kernels: none -> 56 us  [fused_body(): pl.pallas_call(fused_kernel, out_shape=(jax.ShapeDtypeStruct((4, 128, 512...]
    conv_general_dilated x2 -> x0, matrix products: 43 us -> none  [the longest x1 32.6 us: body(): lax.conv_general_dilated(per_channel, cotangent, (1, 1, 1), 'VALID', dime...]
    psum x1 -> x0, waiting for transfers between devices: 17.5 us -> none  [body(): summed = lax.psum(term, 'depth')]
    all_gather x1 -> x0, waiting for transfers between devices: 17.5 us -> none  [body(): piece = lax.all_gather(weights, 'filt', axis=0, tiled=True)]
    ppermute x4 -> x0, waiting for transfers between devices: 11.8 us -> none  [the longest x2 9.88 us: padded_2(): lax.ppermute(lax.slice_in_dim(block, block.shape[dim] - width, None, axis...]
    ppermute x4 -> x0, starting transfers between devices: 8.74 us -> none  [the longest x2 6.16 us: padded_2(): lax.ppermute(lax.slice_in_dim(block, block.shape[dim] - width, None, axis...]
    conv_general_dilated x4 -> x0, local copies, waits for them, and re-layouts: 7.27 us -> none  [body(): lax.conv_general_dilated(stacked, kernel, (1, 1, 1), 'VALID', dimension_n...]
  transfers between devices with their start and end apart: 7 -> 0, of which waited for: 5 -> 0; matrix products, arithmetic and copies ran while one was open for 28% -> 0% of each run, Pallas kernels for 0% -> 0%
where the time goes in v1:
time: 62.3 us; the launch traced here: 62.1 us
  Pallas kernels  56 us (90%)
  local copies, waits for them, and re-layouts  5.35 us (9%)
  between operations  0.71 us (1%)
    pallas_call x1, Pallas kernels, fused_body(): pl.pallas_call(fused_kernel, out_shape=(jax.ShapeDtypeStruct((4, 128, 512...  56 us
    reshape x2, local copies, waits for them, and re-layouts, fused_body(): v = volume.transpose(1, 0, 2, 3).reshape(4, 256, 512)  1.7 us
    unnamed x6, local copies, waits for them, and re-layouts  1.48 us

profile of v1, /device:TPU:0, one launch (start us, length us, event | category | flops | bytes accessed | tf_op | source)
XLA Modules:
  0.0 62.1 jit_solution(2524978267897688004)
XLA Ops:
  0.6 0.0 copy-start
  0.6 1.5 %reshape.29 = bf16[4,256,512]{2,0,1:T(4,128)(2,1)S(1)} reshape(bf16[4,256,4,128]{3,2,0,1:T(4,128)(2,1)} %bitcast.21) | data formatting | bytes 2097152 | tf_op jit(solution)/shard_map/reshape | solution.py:324
  2.2 0.0 copy-start.1
  2.2 0.2 copy.15.v_ref
  2.4 0.8 %copy-done.1 = bf16[128,4,4,128]{3,2,1,0:T(4,128)(2,1)S(1)} copy-done((bf16[128,4,4,128]{3,2,1,0:T(4,128)(2,1)S(1)}, bf16[128,4,4,128]{3,2,1,0:T(4,128)(2,1)}, u32[]{:S(2)}) %copy-start.1) | copy-done | bytes 524312
  3.2 0.2 reshape.30
  3.4 0.1 copy.16.g_ref
  3.5 0.0 copy-done
  3.5 0.0 copy-start.2
  3.5 0.6 %copy-done.2 = f32[128]{0:T(128)S(1)} copy-done((f32[128]{0:T(128)S(1)}, f32[128]{0:T(128)}, u32[]{:S(2)}) %copy-start.2) | copy-done | bytes 536
  4.2 0.1 broadcast_in_dim.2.b_ref
  4.2 56.0 %shard_map.59 = (bf16[4,128,512]{2,1,0:T(8,128)(2,1)S(1)}, f32[2,27,8,128]{3,2,1,0:T(8,128)S(1)}) custom-call(bf16[4,256,512]{2,1,0:T(8,128)(2,1)S(1)} %copy.15.v_ref, bf16[2,216,128]{2,1,0:T(8,128)(2,1)S(1)} %copy_bitcast_fusion.2.w_ref, f32[128,128]{1,0:T(8,128)S(1)} %broadcast_in_dim.2.b_ref, bf16[4,128,512]{2,1,0:T(8,128)(2,1)S(1)} %copy.16.g_ref), custom_call_target="tpu_custom_call" | custom-call | tf_op jit(solution)/shard_map/pallas_call | solution.py:330
  60.3 0.1 reshape.27
  60.4 1.0 %copy.20 = bf16[4,128,4,128]{3,2,0,1:T(4,128)(2,1)} copy(bf16[4,128,4,128]{3,2,1,0:T(4,128)(2,1)S(1)} %reshape.27) | data formatting | bytes 1048576 | tf_op jit(solution)/shard_map/reshape | solution.py:356
  61.4 0.7 %copy_bitcast_fusion.1 = f32[8,27,256]{2,0,1:T(8,128)} fusion(f32[2,27,8,128]{3,2,1,0:T(8,128)S(1)} %get-tuple-element.5), kind=kLoop, calls=%fused_computation.1 | loop fusion | bytes 442368 | tf_op jit(solution)/shard_map/reshape | solution.py:357
  (1 shorter events, 0.0 us)
Async XLA Ops:
  0.6 2.9 %copy-start = (bf16[8,27,256]{2,0,1:T(8,128)(2,1)S(1)}, bf16[8,27,256]{2,0,1:T(8,128)(2,1)}, u32[]{:S(2)}) copy-start(bf16[8,27,256]{2,0,1:T(8,128)(2,1)} %param.5) | copy-start | bytes 331780
  2.2 1.0 %copy-start.1 = (bf16[128,4,4,128]{3,2,1,0:T(4,128)(2,1)S(1)}, bf16[128,4,4,128]{3,2,1,0:T(4,128)(2,1)}, u32[]{:S(2)}) copy-start(bf16[128,4,4,128]{3,2,1,0:T(4,128)(2,1)} %param.7) | copy-start | bytes 1572868
  3.5 0.7 %copy-start.2 = (f32[128]{0:T(128)S(1)}, f32[128]{0:T(128)}, u32[]{:S(2)}) copy-start(f32[128]{0:T(128)} %param.6) | copy-start | bytes 1540

commit v2 on v1

v2 whole, which is shorter than its diff:
```python
import jax
import jax.numpy as jnp
from jax import lax
from jax.experimental import pallas as pl
from jax.experimental.pallas import tpu as pltpu
from jax.sharding import PartitionSpec as P

F32 = jnp.float32
BF16 = jnp.bfloat16
Y_FIRST = (1, 4, 7)
MESH = pl.DeviceIdType.MESH


def padded_2(block, sides, width):
    for axis, dim in sides:
        count = lax.axis_size(axis)
        forward = [(i, i + 1) for i in range(count - 1)]
        backward = [(target, source) for source, target in forward]
        low = lax.ppermute(
            lax.slice_in_dim(block, block.shape[dim] - width, None, axis=dim), axis, forward
        )
        high = lax.ppermute(lax.slice_in_dim(block, 0, width, axis=dim), axis, backward)
        block = jnp.concatenate([low, block, high], axis=dim)
    return block


def general_body(volume, weights, bias, grad_out):
    channels = volume.shape[0]
    rimmed = padded_2(volume, (("filt", 2), ("depth", 1)), 1)
    padded = jnp.pad(rimmed, ((0, 0), (0, 0), (0, 0), (1, 1)))
    stacked = padded[None]
    per_channel = padded[:, None]
    piece = lax.all_gather(weights, "filt", axis=0, tiled=True)
    count = piece.shape[0]
    kernel = piece.reshape(count, 3, 3, 3, channels)
    result = lax.conv_general_dilated(
        stacked,
        kernel,
        (1, 1, 1),
        "VALID",
        dimension_numbers=("NCDHW", "ODHWI", "NCDHW"),
        preferred_element_type=jnp.float32,
    )
    output = (result[0] + bias[:, None, None, None]).astype(jnp.bfloat16)
    all_filters = grad_out.shape[0]
    taps = lax.conv_general_dilated(
        per_channel,
        grad_out[:, None],
        (1, 1, 1),
        "VALID",
        dimension_numbers=("NCDHW", "OIDHW", "CDHWN"),
        preferred_element_type=jnp.float32,
    )
    term = taps.reshape(all_filters, 27, channels)
    summed = lax.psum(term, "depth")
    grad_w = lax.psum_scatter(summed, "filt", scatter_dimension=0, tiled=True)
    return (output, grad_w)


def fused_kernel(
    v_ref, w_ref, b_ref, g_ref,
    out_ref, gw_ref,
    vp, g3, wg, w9, part, ra, b1, b2, b3, gs,
    hs, hr, ws, wr, rs_s, rs_r, zs, zr,
):
    me = lax.axis_index("filt")
    core = lax.axis_index("depth")
    other = 1 - core
    xi = me % 2
    yi = (me // 2) % 2
    zi = me // 4
    x_peer = me + 1 - 2 * xi
    y_peer = me + 2 - 4 * yi
    z_to = [(zi + k) % 4 for k in (1, 2, 3)]
    z_peer = [t * 4 + yi * 2 + xi for t in z_to]
    left, right = me - 1, me + 1

    def dev(filt, depth=None):
        return {"filt": filt, "depth": core if depth is None else depth}

    def copy(src, dst, s_sem, r_sem, device):
        return pltpu.make_async_remote_copy(
            src_ref=src, dst_ref=dst, send_sem=s_sem, recv_sem=r_sem,
            device_id=device, device_id_type=MESH,
        )

    barrier = pltpu.get_barrier_semaphore()

    def greet(device):
        pl.semaphore_signal(barrier, inc=1, device_id=device, device_id_type=MESH)

    greet(dev(me, other))
    greet(dev(x_peer))
    greet(dev(y_peer))
    for p in z_peer:
        greet(dev(p))

    @pl.when(me > 0)
    def _():
        greet(dev(left))

    @pl.when(me < 15)
    def _():
        greet(dev(right))

    pl.semaphore_wait(barrier, 6 + jnp.minimum(me, 1) + jnp.minimum(15 - me, 1))

    w_x = copy(w_ref.at[core], wg.at[core, yi, zi, xi], ws.at[3], wr.at[3], dev(x_peer))
    w_x.start()
    wg[core, yi, zi, xi] = w_ref[core]

    to_right = copy(v_ref.at[:, 3], vp.at[1:5, 0], hs.at[0], hr.at[0], dev(right))
    to_left = copy(v_ref.at[:, 0], vp.at[1:5, 5], hs.at[1], hr.at[1], dev(left))

    @pl.when(me < 15)
    def _():
        to_right.start()

    @pl.when(me > 0)
    def _():
        to_left.start()

    my_edge = 3 - 3 * core
    there = 5 * core
    send_slot = 5 - 5 * other
    inner = copy(v_ref.at[my_edge], vp.at[send_slot, 1:5], hs.at[2], hr.at[2], dev(me, other))
    inner.start()

    vp[1:5, 1:5] = v_ref[...]
    empty = 5 - 5 * (1 - core)
    vp[empty] = jnp.zeros((6, 256, 128), BF16)

    @pl.when(me == 0)
    def _():
        vp[1:5, 0] = jnp.zeros((4, 256, 128), BF16)
        vp[send_zero_slot(core), 0] = jnp.zeros((256, 128), BF16)

    @pl.when(me == 15)
    def _():
        vp[1:5, 5] = jnp.zeros((4, 256, 128), BF16)
        vp[send_zero_slot(core), 5] = jnp.zeros((256, 128), BF16)

    lane = lax.broadcasted_iota(jnp.int32, (128, 128), 1)
    for z in range(4):
        for x in range(4):
            cols = slice(x * 128, x * 128 + 128)
            g = g_ref[z, x]
            gf = g.astype(F32)
            up = jnp.where(lane == 127, 0.0, pltpu.roll(gf, 127, 1))
            down = jnp.where(lane == 0, 0.0, pltpu.roll(gf, 1, 1))
            g3[z, 0:128, cols] = up.astype(BF16)
            g3[z, 128:256, cols] = g
            g3[z, 256:384, cols] = down.astype(BF16)

    w_z = [
        copy(wg.at[core, yi, zi], wg.at[core, yi, zi], ws.at[k], wr.at[k], dev(z_peer[k]))
        for k in range(3)
    ]
    w_y = copy(wg.at[core, yi], wg.at[core, yi], ws.at[4], wr.at[4], dev(y_peer))
    w_c = copy(wg.at[core], wg.at[core], ws.at[5], wr.at[5], dev(me, other))

    def grad(j):
        dz, dx = j // 3, j % 3
        total = None
        for z in range(4):
            term = lax.dot_general(
                g3[z], jnp.concatenate([vp[z + dz, dx + x] for x in range(4)], axis=1),
                (((1,), (1,)), ((), ())), preferred_element_type=F32,
            )
            total = term if total is None else total + term
        for h in range(2):
            blocks = total[:, h * 128 : h * 128 + 128].reshape(3, 4, 2, 2, 8, 128)
            for y in range(2):
                for x in range(2):
                    for dy in range(3):
                        first, second = (x, y) if j not in Y_FIRST else (y, x)
                        part[j, h, first, second, :, dy] = blocks[dy, :, y, x]

    def stage_a(j):
        return copy(part.at[j, other], ra.at[j], rs_s.at[0, j], rs_r.at[0, j], dev(me, other))

    def path(j):
        return ((xi, x_peer), (yi, y_peer)) if j not in Y_FIRST else ((yi, y_peer), (xi, x_peer))

    def stage_1(j):
        side, peer = path(j)[0]
        return copy(ra.at[j, 1 - side], b1.at[j], rs_s.at[1, j], rs_r.at[1, j], dev(peer))

    def stage_2(j):
        side, peer = path(j)[1]
        return copy(b1.at[j, 1 - side], b2.at[j], rs_s.at[2, j], rs_r.at[2, j], dev(peer))

    def stage_3(j):
        return [
            copy(b2.at[j, z_to[k]], b3.at[j, k], zs.at[j, k], zr.at[j, k], dev(z_peer[k]))
            for k in range(3)
        ]

    def after_a(j):
        stage_a(j).wait_recv()
        ra[j] = ra[j] + part[j, core]
        stage_1(j).start()

    def after_1(j):
        stage_1(j).wait_recv()
        b1[j] = b1[j] + ra[j, path(j)[0][0]]
        stage_2(j).start()

    def after_2(j):
        stage_2(j).wait_recv()
        b2[j] = b2[j] + b1[j, path(j)[1][0]]
        for c in stage_3(j):
            c.start()

    def after_3(j):
        for c in stage_3(j):
            c.wait_recv()
        gs[core, 3 * j : 3 * j + 3] = b2[j, zi] + b3[j, 0] + b3[j, 1] + b3[j, 2]

    def arrange():
        for h in range(2):
            for z in range(4):
                for y in range(2):
                    pair = [wg[h, y, z, x].astype(F32).reshape(27, 8, 128) for x in range(2)]
                    rows = jnp.concatenate(pair, axis=1).astype(BF16).reshape(9, 3, 16, 128)
                    at = 16 * (2 * z + y)
                    for dy in range(3):
                        w9[:, dy * 128 + at : dy * 128 + at + 16, h * 128 : h * 128 + 128] = rows[:, dy]

    def forward(u):
        z, half = u // 2, u % 2
        total = None
        for dz in range(3):
            for dx in range(3):
                at = dx + 2 * half
                cells = jnp.concatenate([vp[z + dz, at], vp[z + dz, at + 1]], axis=1)
                term = jnp.dot(w9[dz * 3 + dx], cells, preferred_element_type=F32)
                total = term if total is None else total + term
        for x in range(2):
            cols = slice(x * 128, x * 128 + 128)
            low = jnp.where(lane == 0, 0.0, pltpu.roll(total[0:128, cols], 1, 1))
            high = jnp.where(lane == 127, 0.0, pltpu.roll(total[256:384, cols], 127, 1))
            value = low + total[128:256, cols] + high + b_ref[...]
            out_ref[z, x + 2 * half] = value.astype(BF16)

    edge_slot = 4 - 3 * core
    corner_l = copy(vp.at[edge_slot, 0], vp.at[send_slot, 0], hs.at[3], hr.at[3], dev(me, other))
    corner_r = copy(vp.at[edge_slot, 5], vp.at[send_slot, 5], hs.at[4], hr.at[4], dev(me, other))

    def rim():
        @pl.when(me > 0)
        def _():
            to_right.wait_recv()
            corner_l.start()

        @pl.when(me < 15)
        def _():
            to_left.wait_recv()
            corner_r.start()

    def corners():
        @pl.when(me > 0)
        def _():
            corner_l.wait_recv()

        @pl.when(me < 15)
        def _():
            corner_r.wait_recv()

    def chunk(j):
        grad(j)
        stage_a(j).start()

    w_x.wait_recv()
    for c in w_z:
        c.start()
    inner.wait_recv()
    chunk(1)
    chunk(4)
    after_a(1)
    chunk(7)
    after_a(4)
    after_a(7)
    after_1(1)
    after_1(4)
    rim()
    chunk(3)
    chunk(5)
    after_a(3)
    for c in w_z:
        c.wait_recv()
    w_y.start()
    after_a(5)
    after_1(7)
    corners()
    chunk(0)
    chunk(2)
    after_a(0)
    chunk(6)
    after_a(2)
    chunk(8)
    after_a(6)
    after_a(8)
    after_2(1)
    after_2(4)
    after_1(3)
    after_2(7)
    after_1(5)
    after_3(1)
    after_2(3)
    after_1(0)
    after_2(5)
    after_3(4)
    w_y.wait_recv()
    w_c.start()
    after_1(2)
    after_2(0)
    after_3(7)
    w_c.wait_recv()
    arrange()
    forward(0)
    after_1(6)
    after_2(2)
    after_3(3)
    forward(1)
    forward(2)
    after_1(8)
    after_2(6)
    forward(3)
    after_3(5)
    forward(4)
    after_2(8)
    forward(5)
    after_3(0)
    forward(6)
    after_3(2)
    forward(7)
    after_3(6)
    after_3(8)
    last = copy(gs.at[core], gs.at[core], hs.at[5], hr.at[5], dev(me, other))
    last.start()

    @pl.when(me < 15)
    def _():
        to_right.wait_send()
        corner_r.wait_send()

    @pl.when(me > 0)
    def _():
        to_left.wait_send()
        corner_l.wait_send()

    inner.wait_send()
    for c in w_z + [w_y, w_x, w_c]:
        c.wait_send()
    for j in range(9):
        stage_a(j).wait_send()
        stage_1(j).wait_send()
        stage_2(j).wait_send()
        for c in stage_3(j):
            c.wait_send()
    last.wait()
    for h in range(2):
        gw_ref[:, :, h * 128 : h * 128 + 128] = gs[h]


def send_zero_slot(core):
    return 5 - 5 * core


def fused_body(volume, weights, bias, grad_out):
    v = volume.transpose(1, 2, 0, 3)
    g = grad_out.transpose(1, 2, 0, 3)
    w = weights.reshape(8, 27, 2, 128).transpose(2, 1, 0, 3).reshape(2, 216, 128)
    b = jnp.broadcast_to(bias[:, None], (128, 128))
    vmem = pl.BlockSpec(memory_space=pltpu.VMEM)
    dma = pltpu.SemaphoreType.DMA
    out, gw = pl.pallas_call(
        fused_kernel,
        out_shape=(
            jax.ShapeDtypeStruct((4, 4, 128, 128), BF16),
            jax.ShapeDtypeStruct((27, 8, 256), F32),
        ),
        in_specs=[vmem] * 4,
        out_specs=(vmem, vmem),
        scratch_shapes=[
            pltpu.VMEM((6, 6, 256, 128), BF16),
            pltpu.VMEM((4, 384, 512), BF16),
            pltpu.VMEM((2, 2, 4, 2, 216, 128), BF16),
            pltpu.VMEM((9, 384, 256), BF16),
            pltpu.VMEM((9, 2, 2, 2, 4, 3, 8, 128), F32),
            pltpu.VMEM((9, 2, 2, 4, 3, 8, 128), F32),
            pltpu.VMEM((9, 2, 4, 3, 8, 128), F32),
            pltpu.VMEM((9, 4, 3, 8, 128), F32),
            pltpu.VMEM((9, 3, 3, 8, 128), F32),
            pltpu.VMEM((2, 27, 8, 128), F32),
            dma((6,)), dma((6,)), dma((6,)), dma((6,)),
            dma((3, 9)), dma((3, 9)), dma((9, 3)), dma((9, 3)),
        ],
        compiler_params=pltpu.CompilerParams(
            collective_id=0, has_side_effects=True, vmem_limit_bytes=48 << 20
        ),
    )(v, w, b, g)
    output = out.transpose(2, 0, 1, 3)
    grad_w = gw.transpose(1, 0, 2)
    return (output, grad_w)


def solution(mesh):
    in_specs = (
        P(None, "depth", "filt", None),
        P("filt", None, None),
        P(),
        P(None, "depth", "filt", None),
    )
    out_specs = (P(None, "depth", "filt", None), P("filt", None, None))
    small = mesh.shape["filt"] == 16 and mesh.shape["depth"] == 2

    def body(volume, weights, bias, grad_out):
        shapes = (volume.shape, weights.shape, grad_out.shape)
        if small and shapes == ((256, 4, 4, 128), (8, 27, 256), (128, 4, 4, 128)):
            return fused_body(volume, weights, bias, grad_out)
        return general_body(volume, weights, bias, grad_out)

    return jax.shard_map(body, mesh=mesh, in_specs=in_specs, out_specs=out_specs, check_vma=False)
```

time: 62.3 us -> 58.1 us (0.933)
  Pallas kernels: 56 us -> 53 us
  local copies, waits for them, and re-layouts: 5.35 us -> 4.23 us
    reshape x7 -> x0, local copies, waits for them, and re-layouts: 3.79 us -> none  [the longest x2 1.7 us: fused_body(): v = volume.transpose(1, 0, 2, 3).reshape(4, 256, 512)]
    pallas_call x1, Pallas kernels: 56 us -> 53 us  [fused_body(): pl.pallas_call(fused_kernel, out_shape=(jax.ShapeDtypeStruct((4, 4, 128,...]
    unnamed x6 -> x8, local copies, waits for them, and re-layouts: 1.48 us -> 3.4 us
    broadcast_in_dim x1, local copies, waits for them, and re-layouts: 0.07 us -> 0.82 us  [fused_body(): b = jnp.broadcast_to(bias[:, None], (128, 128))]
where the time goes in v2:
time: 58.1 us; the launch traced here: 57.9 us
  Pallas kernels  53 us (91%)
  local copies, waits for them, and re-layouts  4.23 us (7%)
  between operations  0.68 us (1%)
    pallas_call x1, Pallas kernels, fused_body(): pl.pallas_call(fused_kernel, out_shape=(jax.ShapeDtypeStruct((4, 4, 128,...  53 us
    unnamed x8, local copies, waits for them, and re-layouts  3.4 us

profile of v2, /device:TPU:0, one launch (start us, length us, event | category | flops | bytes accessed | tf_op | source)
XLA Modules:
  0.0 57.9 jit_solution(11458062678242088993)
XLA Ops:
  0.6 0.0 copy-start
  0.6 0.0 copy-start.1
  0.7 0.8 %broadcast_in_dim.2.b_ref = f32[128,128]{1,0:T(8,128)S(1)} broadcast(f32[128]{0:T(128)} %param.6), dimensions={0} | broadcast | bytes 66048 | tf_op jit(solution)/shard_map/broadcast_in_dim | solution.py:375
  1.5 0.1 copy-done
  1.5 1.2 %copy.14 = bf16[128,4,4,128]{3,0,2,1:T(8,128)(2,1)S(1)} copy(bf16[128,4,4,128]{3,2,1,0:T(4,128)(2,1)} %param.7) | data formatting | bytes 1048576 | tf_op args[3]
  2.7 0.0 copy-done.1
  2.7 0.3 copy.13
  3.0 53.0 %shard_map.59 = (bf16[4,4,128,128]{3,2,1,0:T(8,128)(2,1)S(1)}, f32[27,8,256]{2,1,0:T(8,128)S(1)}) custom-call(bf16[4,4,256,128]{3,2,1,0:T(8,128)(2,1)S(1)} %bitcast.15, bf16[2,216,128]{2,1,0:T(8,128)(2,1)S(1)} %copy_bitcast_fusion.2.w_ref, f32[128,128]{1,0:T(8,128)S(1)} %broadcast_in_dim.2.b_ref, bf16[4,4,128,128]{3,2,1,0:T(8,128)(2,1)S(1)} %bitcast.16), custom_call_target="tpu_custom_call" | custom-call | tf_op jit(solution)/shard_map/pallas_call | solution.py:378
  56.0 1.2 %copy.9 = bf16[128,4,4,128]{3,2,1,0:T(4,128)(2,1)} copy(bf16[128,4,4,128]{3,0,2,1:T(8,128)(2,1)S(1)} %bitcast.17) | data formatting | bytes 1048576
  57.2 0.7 %copy.16 = f32[8,27,256]{2,0,1:T(8,128)} copy(f32[8,27,256]{2,0,1:T(8,128)S(1)} %bitcast.18) | data formatting | bytes 442368
  (1 shorter events, 0.0 us)
Async XLA Ops:
  0.6 0.9 %copy-start = (bf16[8,27,256]{2,0,1:T(8,128)(2,1)S(1)}, bf16[8,27,256]{2,0,1:T(8,128)(2,1)}, u32[]{:S(2)}) copy-start(bf16[8,27,256]{2,0,1:T(8,128)(2,1)} %param.5) | copy-start | bytes 331780
  0.6 2.1 %copy-start.1 = (bf16[256,4,4,128]{3,2,1,0:T(4,128)(2,1)S(1)}, bf16[256,4,4,128]{3,2,1,0:T(4,128)(2,1)}, u32[]{:S(2)}) copy-start(bf16[256,4,4,128]{3,2,1,0:T(4,128)(2,1)} %param.4) | copy-start | bytes 3145732

commit v3 on v2

--- a/solution.py
+++ b/solution.py
@@ -157,7 +157,10 @@
         for k in range(3)
     ]
     w_y = copy(wg.at[core, yi], wg.at[core, yi], ws.at[4], wr.at[4], dev(y_peer))
-    w_c = copy(wg.at[core], wg.at[core], ws.at[5], wr.at[5], dev(me, other))
+    w_c = [
+        copy(wg.at[core, row], wg.at[core, row], ws.at[5 + k], wr.at[5 + k], dev(me, other))
+        for k, row in enumerate((yi, 1 - yi))
+    ]
 
     def grad(j):
         dz, dx = j // 3, j % 3
@@ -290,6 +293,7 @@
     for c in w_z:
         c.wait_recv()
     w_y.start()
+    w_c[0].start()
     after_a(5)
     after_1(7)
     corners()
@@ -312,11 +316,12 @@
     after_2(5)
     after_3(4)
     w_y.wait_recv()
-    w_c.start()
+    w_c[1].start()
     after_1(2)
     after_2(0)
     after_3(7)
-    w_c.wait_recv()
+    for c in w_c:
+        c.wait_recv()
     arrange()
     forward(0)
     after_1(6)
@@ -351,7 +356,7 @@
         corner_l.wait_send()
 
     inner.wait_send()
-    for c in w_z + [w_y, w_x, w_c]:
+    for c in w_z + [w_y, w_x] + w_c:
         c.wait_send()
     for j in range(9):
         stage_a(j).wait_send()
@@ -394,7 +399,7 @@
             pltpu.VMEM((9, 4, 3, 8, 128), F32),
             pltpu.VMEM((9, 3, 3, 8, 128), F32),
             pltpu.VMEM((2, 27, 8, 128), F32),
-            dma((6,)), dma((6,)), dma((6,)), dma((6,)),
+            dma((6,)), dma((6,)), dma((7,)), dma((7,)),
             dma((3, 9)), dma((3, 9)), dma((9, 3)), dma((9, 3)),
         ],
         compiler_params=pltpu.CompilerParams(

time: 58.1 us -> 57.7 us (level)
  no operation moved by 1% of the time
where the time goes in v3:
time: 57.7 us; the launch traced here: 57.5 us
  Pallas kernels  52.6 us (91%)
  local copies, waits for them, and re-layouts  4.23 us (7%)
  between operations  0.68 us (1%)
    pallas_call x1, Pallas kernels, fused_body(): pl.pallas_call(fused_kernel, out_shape=(jax.ShapeDtypeStruct((4, 4, 128,...  52.6 us
    unnamed x8, local copies, waits for them, and re-layouts  3.4 us

profile of v3, /device:TPU:0, one launch (start us, length us, event | category | flops | bytes accessed | tf_op | source)
XLA Modules:
  0.0 57.5 jit_solution(3363982110832778719)
XLA Ops:
  0.6 0.0 copy-start
  0.6 0.0 copy-start.1
  0.7 0.8 %broadcast_in_dim.2.b_ref = f32[128,128]{1,0:T(8,128)S(1)} broadcast(f32[128]{0:T(128)} %param.6), dimensions={0} | broadcast | bytes 66048 | tf_op jit(solution)/shard_map/broadcast_in_dim | solution.py:380
  1.5 0.1 copy-done
  1.5 1.2 %copy.14 = bf16[128,4,4,128]{3,0,2,1:T(8,128)(2,1)S(1)} copy(bf16[128,4,4,128]{3,2,1,0:T(4,128)(2,1)} %param.7) | data formatting | bytes 1048576 | tf_op args[3]
  2.7 0.0 copy-done.1
  2.7 0.3 copy.13
  3.0 52.6 %shard_map.59 = (bf16[4,4,128,128]{3,2,1,0:T(8,128)(2,1)S(1)}, f32[27,8,256]{2,1,0:T(8,128)S(1)}) custom-call(bf16[4,4,256,128]{3,2,1,0:T(8,128)(2,1)S(1)} %bitcast.15, bf16[2,216,128]{2,1,0:T(8,128)(2,1)S(1)} %copy_bitcast_fusion.2.w_ref, f32[128,128]{1,0:T(8,128)S(1)} %broadcast_in_dim.2.b_ref, bf16[4,4,128,128]{3,2,1,0:T(8,128)(2,1)S(1)} %bitcast.16), custom_call_target="tpu_custom_call" | custom-call | tf_op jit(solution)/shard_map/pallas_call | solution.py:383
  55.6 1.2 %copy.9 = bf16[128,4,4,128]{3,2,1,0:T(4,128)(2,1)} copy(bf16[128,4,4,128]{3,0,2,1:T(8,128)(2,1)S(1)} %bitcast.17) | data formatting | bytes 1048576
  56.8 0.7 %copy.16 = f32[8,27,256]{2,0,1:T(8,128)} copy(f32[8,27,256]{2,0,1:T(8,128)S(1)} %bitcast.18) | data formatting | bytes 442368
  (1 shorter events, 0.0 us)
Async XLA Ops:
  0.6 0.9 %copy-start = (bf16[8,27,256]{2,0,1:T(8,128)(2,1)S(1)}, bf16[8,27,256]{2,0,1:T(8,128)(2,1)}, u32[]{:S(2)}) copy-start(bf16[8,27,256]{2,0,1:T(8,128)(2,1)} %param.5) | copy-start | bytes 331780
  0.6 2.1 %copy-start.1 = (bf16[256,4,4,128]{3,2,1,0:T(4,128)(2,1)S(1)}, bf16[256,4,4,128]{3,2,1,0:T(4,128)(2,1)}, u32[]{:S(2)}) copy-start(bf16[256,4,4,128]{3,2,1,0:T(4,128)(2,1)} %param.4) | copy-start | bytes 3145732
